TPU v7x, 128 devices: a whole 4x4x4 slice. The times are simulated.
128 devices in a mesh: row: 8 (over x, core), col: 16 (over y, z).
Axes of the slice: x: 4, y: 4, z: 4, core: 2. Of those that a mesh axis runs over, the one named last changes fastest.
Arguments:
- factor: float32 [4, 8, 1024, 2048], P(None, 'row', None, 'col'), as said below
- cross_cov: float32 [4, 8, 1024, 1024], P(None, 'row', 'col'), may hold values from -6 to 6
Outputs:
- overwritten: float32 [4, 8, 1024, 1024], P(None, 'row', 'col')
Inputs may be any that keep to these rules, and one draw needn't show every extreme that they name: The diagonal entries of the factor lie between 1 and 3.
All inputs are finite; a program needn't handle non-finite values.
Results may differ from a plain program's by a relative error of at most 0.00014.
Values sent between devices are 32-bit elements; how exact they have to be, the bound alone decides.
No kernel may reach another device: no remote copies, remote signals or barrier semaphores. Data moves between devices by JAX's collectives and lax.ppermute only.
A program may use at most 128 MiB of HBM per device.

v0:
```python
import jax
import jax.numpy as jnp
from jax import lax
from jax.sharding import PartitionSpec as P


def broadcast(x, axis, root):
    mine = lax.axis_index(axis) == root
    return lax.psum(jnp.where(mine, x, jnp.zeros_like(x)), axis)


def spread(block, root):
    return broadcast(block, "row", root)


def reduce_turn(partial_value):
    return lax.psum_scatter(partial_value, "col", scatter_dimension=0, tiled=True)


def shards(factor, cross_cov):
    col_id = lax.axis_index("col")
    row_id = lax.axis_index("row")
    lead_rows = factor[0, 0]
    own_rhs = cross_cov[0, 0]
    block_row, block_rhs = (
        lax.all_gather(lead_rows, "col", axis=1, tiled=True),
        lax.all_gather(own_rhs, "col", axis=0, tiled=True),
    )
    block_size = block_row.shape[0]
    first_block = lax.linalg.triangular_solve(
        block_row[:, :block_size], block_rhs, left_side=True, lower=True
    )
    first_block = spread(first_block, 0)
    second_rhs = block_rhs - jnp.dot(
        block_row[:, :block_size], first_block, precision=lax.Precision.HIGHEST
    )
    second_block = lax.linalg.triangular_solve(
        block_row[:, block_size:], second_rhs, left_side=True, lower=True
    )
    second_block = spread(second_block, 1)
    solved = jnp.concatenate([first_block, second_block], 0)
    local_factor = factor[:, 0]
    col_width = local_factor.shape[2]
    my_rows = lax.dynamic_slice_in_dim(solved, col_id * col_width, col_width, 0)
    pieces = []
    for turn_id in range(local_factor.shape[0]):
        partial_value = jnp.dot(local_factor[turn_id], my_rows, precision=lax.Precision.HIGHEST)
        pieces.append(reduce_turn(partial_value))
    reduced = jnp.stack(pieces, 0)
    updated = cross_cov[:, 0] - reduced
    slice_rows = own_rhs.shape[0]
    first_piece = lax.dynamic_slice_in_dim(first_block, col_id * slice_rows, slice_rows, 0)
    second_piece = lax.dynamic_slice_in_dim(second_block, col_id * slice_rows, slice_rows, 0)
    head_rows = jnp.where(
        row_id == 0, first_piece, jnp.where(row_id == 1, second_piece, updated[0])
    )
    result = jnp.concatenate([head_rows[None], updated[1:]], 0)
    return result[:, None]


def solution(mesh):
    placed = (P(None, "row", None, "col"), P(None, "row", "col", None))
    return jax.shard_map(
        shards, mesh=mesh, in_specs=placed, out_specs=P(None, "row", "col", None), check_vma=False
    )
```

profile of v0, /device:TPU:0, one launch (start us, length us, event | category | flops | bytes accessed | tf_op | source)
XLA Modules:
  0.0 875.4 jit_solution(348379081481082438)
XLA Ops:
  6.5 1.0 slice.104
  7.5 1.0 copy.20
  8.6 1.9 slice.102
  10.5 53.1 %all-gather.7.cloned.1.call-done = f32[1,1,1024,1024]{3,1,0,2:T(1,128)} async-done(((f32[1,1,64,1024]{3,1,0,2:T(1,128)}), f32[1,1,1024,1024]{3,1,0,2:T(1,128)}) %all-gather.7.cloned.1.call-update) | async-done | bytes 4194320 | tf_op jit(solution)/shard_map/all_gather | solution.py:27
  63.7 11.0 %copy.10 = f32[1,1,1024,1024]{2,3,1,0:T(8,128)} copy(f32[1,1,1024,1024]{3,1,0,2:T(1,128)} %all-gather.7.cloned.1.call-done) | data formatting | bytes 8388608 | tf_op jit(solution)/shard_map/all_gather | solution.py:27
  74.7 69.2 %all-gather.5.cloned.1.call-done = f32[1,1,1024,2048]{3,2,1,0:T(8,128)} async-done(((f32[1,1,1024,128]{3,2,1,0:T(8,128)}), f32[1,1,1024,2048]{3,2,1,0:T(8,128)}) %all-gather.5.cloned.1.call-update) | async-done | bytes 8388624 | tf_op jit(solution)/shard_map/all_gather | solution.py:26
  143.9 8.0 slice_select_fusion
  151.9 22.5 %while.4 = (s32[]{:T(128)}, f32[1024,1024]{1,0:T(8,128)}, s32[8,2]{0,1:T(2,128)S(1)}, f32[8,128,128]{2,1,0:T(8,128)S(1)}, s32[]{:T(128)}) while((s32[]{:T(128)}, f32[1024,1024]{1,0:T(8,128)}, s32[8,2]{0,1:T(2,128)S(1)}, f32[8,128,128]{2,1,0:T(8,128)S(1)}, s32[]{:T(128)}) %tuple.80), condition=%wide.while_cond, body=%wide.while_body.sunk | while | flops 2 | bytes 131181 | solution.py:30
  152.5 2.2 bitcast_dynamic-update-slice_fusion.4
  155.3 2.2 bitcast_dynamic-update-slice_fusion.4
  158.2 2.2 bitcast_dynamic-update-slice_fusion.4
  161.0 2.2 bitcast_dynamic-update-slice_fusion.4
  163.8 2.2 bitcast_dynamic-update-slice_fusion.4
  166.6 2.2 bitcast_dynamic-update-slice_fusion.4
  169.4 2.2 bitcast_dynamic-update-slice_fusion.4
  172.3 2.1 bitcast_dynamic-update-slice_fusion.4
  174.4 78.8 %custom-call.4 = f32[8,128,128]{1,2,0:T(8,128)S(1)} custom-call(f32[8,128,128]{2,1,0:T(8,128)S(1)} %get-tuple-element.20), custom_call_target="InvertDiagBlocksLowerTriangular" | custom-call | tf_op jit(solution)/shard_map/triangular_solve/custom-call.1 | solution.py:30
  253.2 1.9 constant_dynamic-update-slice_fusion.17
  255.1 2.1 convolution_subtract_fusion.9
  257.2 0.8 constant_dynamic-update-slice_fusion.16
  258.0 2.7 convolution_subtract_fusion.1
  261.5 3.7 fusion.36
  265.2 0.8 constant_dynamic-update-slice_fusion.14
  266.0 4.4 fusion.42
  270.4 0.9 constant_dynamic-update-slice_fusion.13
  271.3 5.4 convolution_subtract_fusion.5
  277.4 6.0 convolution_subtract_fusion.3
  284.1 7.5 convolution_subtract_fusion.8
  292.3 2.5 broadcast_select_fusion.1
  294.8 22.5 %while.5 = (s32[]{:T(128)}, f32[1024,1024]{1,0:T(8,128)}, s32[8,2]{0,1:T(2,128)S(1)}, f32[8,128,128]{2,1,0:T(8,128)S(1)}, s32[]{:T(128)}) while((s32[]{:T(128)}, f32[1024,1024]{1,0:T(8,128)}, s32[8,2]{0,1:T(2,128)S(1)}, f32[8,128,128]{2,1,0:T(8,128)S(1)}, s32[]{:T(128)}) %tuple.102), condition=%wide.while_cond.clone, body=%wide.while_body.clone.sunk | while | flops 2 | bytes 131181 | solution.py:37
  295.4 2.2 bitcast_dynamic-update-slice_fusion.5
  298.3 2.2 bitcast_dynamic-update-slice_fusion.5
  301.1 2.2 bitcast_dynamic-update-slice_fusion.5
  303.9 2.2 bitcast_dynamic-update-slice_fusion.5
  306.7 2.2 bitcast_dynamic-update-slice_fusion.5
  309.5 2.2 bitcast_dynamic-update-slice_fusion.5
  312.3 2.2 bitcast_dynamic-update-slice_fusion.5
  315.2 2.1 bitcast_dynamic-update-slice_fusion.5
  317.3 78.6 %custom-call.5 = f32[8,128,128]{1,2,0:T(8,128)S(1)} custom-call(f32[8,128,128]{2,1,0:T(8,128)S(1)} %get-tuple-element.21), custom_call_target="InvertDiagBlocksLowerTriangular" | custom-call | tf_op jit(solution)/shard_map/triangular_solve/custom-call.1 | solution.py:37
  395.9 30.9 %bitcast_subtract_fusion = f32[1024,1024]{0,1:T(8,128)S(1)} fusion(f32[1024,1024]{1,0:T(8,128)} %all-reduce.3.cloned.1.call-done, f32[1024,2048]{1,0:T(8,128)} %bitcast.173, f32[1,1,1024,1024]{2,3,1,0:T(8,128)} %copy.10), kind=kOutput, calls=%fused_computation.7 | convolution fusion | flops 12885950464 | bytes 16777216 | tf_op jit(solution)/shard_map/dot_general | solution.py:34
  426.8 0.8 constant_dynamic-update-slice_fusion.42
  427.6 1.8 convolution_subtract_fusion.7
  429.4 0.8 constant_dynamic-update-slice_fusion.41
  430.2 2.8 convolution_subtract_fusion
  432.9 0.8 constant_dynamic-update-slice_fusion.40
  433.7 3.7 fusion.33
  438.1 4.4 fusion.39
  442.6 0.9 constant_dynamic-update-slice_fusion.38
  443.5 5.4 convolution_subtract_fusion.4
  449.5 6.2 convolution_subtract_fusion.2
  456.3 7.3 convolution_subtract_fusion.6
  464.4 2.5 broadcast_select_fusion
  466.9 71.9 %all-reduce.5.cloned.1.call-done = f32[1024,1024]{1,0:T(8,128)} async-done(((f32[1024,1024]{1,0:T(8,128)}), f32[1024,1024]{1,0:T(8,128)}) %all-reduce.5.cloned.1.call-update) | async-done | bytes 4194320 | tf_op jit(solution)/shard_map/psum | solution.py:9
  538.8 6.2 convolution_bitcast_fusion.3
  545.1 6.1 convolution_bitcast_fusion.2
  551.3 6.1 convolution_bitcast_fusion.1
  557.5 6.2 convolution_bitcast_fusion
  563.7 59.3 %reduce-scatter.5.cloned.1.call-done = f32[64,1024]{1,0:T(8,128)} async-done(((f32[1024,1024]{1,0:T(8,128)}), f32[64,1024]{1,0:T(8,128)}) %reduce-scatter.5.cloned.1.call-update) | async-done | bytes 262160 | tf_op jit(solution)/shard_map/reduce_scatter | solution.py:17
  623.1 80.6 %reduce-scatter.7.cloned.1.call-done = f32[64,1024]{1,0:T(8,128)} async-done(((f32[1024,1024]{1,0:T(8,128)}), f32[64,1024]{1,0:T(8,128)}) %reduce-scatter.7.cloned.1.call-update) | async-done | bytes 262160 | tf_op jit(solution)/shard_map/reduce_scatter | solution.py:17
  703.7 80.4 %reduce-scatter.9.cloned.1.call-done = f32[64,1024]{1,0:T(8,128)} async-done(((f32[1024,1024]{1,0:T(8,128)}), f32[64,1024]{1,0:T(8,128)}) %reduce-scatter.9.cloned.1.call-update) | async-done | bytes 262160 | tf_op jit(solution)/shard_map/reduce_scatter | solution.py:17
  784.0 80.7 %reduce-scatter.11.cloned.1.call-done = f32[64,1024]{1,0:T(8,128)} async-done(((f32[1024,1024]{1,0:T(8,128)}), f32[64,1024]{1,0:T(8,128)}) %reduce-scatter.11.cloned.1.call-update) | async-done | bytes 262160 | tf_op jit(solution)/shard_map/reduce_scatter | solution.py:17
  864.8 1.3 maximum_subtract_fusion
  866.2 1.1 fusion.71
  867.2 1.1 maximum_bitcast_fusion
  (68 shorter events, 15.6 us)
Async XLA Ops:
  6.5 57.1 %all-gather.7.cloned.1.call-start = ((), (), s32[]{:S(2)}) async-start(), calls=%async_computation.11 | async-start | bytes 4456448 | tf_op jit(solution)/shard_map/all_gather | solution.py:27
  8.5 135.4 %all-gather.5.cloned.1.call-start = ((), (), s32[]{:S(2)}) async-start(), calls=%async_computation.10 | async-start | bytes 8912896 | tf_op jit(solution)/shard_map/all_gather | solution.py:26
  10.5 385.5 %all-reduce.3.cloned.1.call-start = ((), (), s32[]{:S(2)}) async-start(), calls=%async_computation.4 | async-start | bytes 8388608 | tf_op jit(solution)/shard_map/psum | solution.py:9
  253.2 4.8 copy-start
  294.7 244.1 %all-reduce.5.cloned.1.call-start = ((), (), s32[]{:S(2)}) async-start(), calls=%async_computation.5 | async-start | bytes 8388608 | tf_op jit(solution)/shard_map/psum | solution.py:9
  466.8 72.0 %copy-start.1 = (f32[4,1,1024,128]{3,2,1,0:T(8,128)S(1)}, f32[4,1,1024,128]{3,2,1,0:T(8,128)}, u32[]{:S(2)}) copy-start(f32[4,1,1024,128]{3,2,1,0:T(8,128)} %param.4) | copy-start | bytes 6291460
  466.8 156.2 %reduce-scatter.5.cloned.1.call-start = ((), (), s32[]{:S(2)}) async-start(), calls=%async_computation.6 | async-start | bytes 4456448 | tf_op jit(solution)/shard_map/reduce_scatter | solution.py:17
  545.0 158.6 %reduce-scatter.7.cloned.1.call-start = ((), (), s32[]{:S(2)}) async-start(), calls=%async_computation.7 | async-start | bytes 4456448 | tf_op jit(solution)/shard_map/reduce_scatter | solution.py:17
  551.2 232.8 %reduce-scatter.9.cloned.1.call-start = ((), (), s32[]{:S(2)}) async-start(), calls=%async_computation.8 | async-start | bytes 4456448 | tf_op jit(solution)/shard_map/reduce_scatter | solution.py:17
  557.4 307.3 %reduce-scatter.11.cloned.1.call-start = ((), (), s32[]{:S(2)}) async-start(), calls=%async_computation.9 | async-start | bytes 4456448 | tf_op jit(solution)/shard_map/reduce_scatter | solution.py:17
  563.7 301.1 %copy-start.2 = (f32[4,1,64,1024]{3,2,1,0:T(8,128)S(1)}, f32[4,1,64,1024]{3,2,1,0:T(8,128)}, u32[]{:S(2)}) copy-start(f32[4,1,64,1024]{3,2,1,0:T(8,128)} %param.5) | copy-start | bytes 3145732
Sparse Core Ops, SparseCore 0:
  9.5 54.1 all-gather.6
  65.8 78.0 all-gather.4
  294.9 73.0 all-reduce.2
  467.0 71.7 all-reduce.4
  545.1 77.8 reduce-scatter.4
  626.6 77.0 reduce-scatter.6
  707.0 76.9 reduce-scatter.8
  787.7 77.0 reduce-scatter.10
where the time goes:
time: 880 us; the launch traced here: 875 us
  waiting for transfers between devices  495 us (56%)
  other arithmetic  174 us (20%)
  matrix products  132 us (15%)
  local copies, waits for them, and re-layouts  59.6 us (7%)
  between operations  14.1 us (2%)
    reduce_scatter x4, waiting for transfers between devices, reduce_turn(): lax.psum_scatter(partial_value, 'col', scatter_dimension=0, tiled=True)  301 us
    another operation x2, other arithmetic, shards(): lax.linalg.triangular_solve(block_row[:, block_size:], second_rhs, left_s...  86.6 us
    another operation x2, other arithmetic, shards(): lax.linalg.triangular_solve(block_row[:, :block_size], block_rhs, left_si...  78.8 us
    psum x2, waiting for transfers between devices, broadcast(): return lax.psum(jnp.where(mine, x, jnp.zeros_like(x)), axis)  71.9 us
    all_gather x1, waiting for transfers between devices, shards(): lax.all_gather(lead_rows, 'col', axis=1, tiled=True)  69.2 us
    all_gather x1, waiting for transfers between devices, shards(): lax.all_gather(own_rhs, 'col', axis=0, tiled=True)  53.1 us
    another operation x15, matrix products, shards(): lax.linalg.triangular_solve(block_row[:, :block_size], block_rhs, left_si...  38.9 us
    another operation x15, matrix products, shards(): lax.linalg.triangular_solve(block_row[:, block_size:], second_rhs, left_s...  37.4 us
  transfers between devices with their start and end apart: 8, of which 7 were waited for; matrix products, arithmetic and copies ran while one was open for 15% of the time, Pallas kernels for 0%

commit v1 on v0

--- a/solution.py
+++ b/solution.py
@@ -2,6 +2,7 @@
 import jax.numpy as jnp
 from jax import lax
 from jax.sharding import PartitionSpec as P
+from jax.lax import axis_index, axis_size, ppermute
 
 
 def broadcast(x, axis, root):
@@ -18,12 +19,35 @@
 
 
 def shards(factor, cross_cov):
+
+    def see_limits_over_axis(point, where_dim):
+        v_now, later, y2 = (axis_size("col"), axis_index("col"), point.shape[where_dim])
+        rack = tuple(((kk, (kk + 1) % v_now) for kk in range(v_now)))
+        opened = jnp.zeros(
+            (*point.shape[:where_dim], v_now * y2, *point.shape[where_dim + 1 :]), point.dtype
+        )
+        row_list = tuple(((kk, (kk - 1) % v_now) for kk in range(v_now)))
+        opened = lax.dynamic_update_slice_in_dim(opened, point, later * y2, axis=where_dim)
+        earlier = v_now // 2
+        all_rows = shaped = point
+        for num in range(1, earlier + 1):
+            all_rows = ppermute(all_rows, "col", rack)
+            opened = lax.dynamic_update_slice_in_dim(
+                opened, all_rows, (later - num) % v_now * y2, axis=where_dim
+            )
+            if num < v_now - earlier:
+                shaped = ppermute(shaped, "col", row_list)
+                opened = lax.dynamic_update_slice_in_dim(
+                    opened, shaped, (later + num) % v_now * y2, axis=where_dim
+                )
+        return opened
+
     col_id = lax.axis_index("col")
     row_id = lax.axis_index("row")
     lead_rows = factor[0, 0]
     own_rhs = cross_cov[0, 0]
     block_row, block_rhs = (
-        lax.all_gather(lead_rows, "col", axis=1, tiled=True),
+        see_limits_over_axis(lead_rows, 1),
         lax.all_gather(own_rhs, "col", axis=0, tiled=True),
     )
     block_size = block_row.shape[0]

time: 880 us -> 839 us (0.953)
  waiting for transfers between devices: 495 us -> 435 us
  matrix products: 132 us -> 88.3 us
  starting transfers between devices: 0.29 us -> 41.1 us
  local copies, waits for them, and re-layouts: 59.6 us -> 77.9 us
    all_gather x1 -> x0, waiting for transfers between devices: 69.2 us -> none  [shards(): lax.all_gather(lead_rows, 'col', axis=1, tiled=True)]
    ppermute x0 -> x15, waiting for transfers between devices: none -> 64.8 us  [the longest x8 54.8 us: see_limits_over_axis(): all_rows = ppermute(all_rows, 'col', rack)]
    all_gather x1, waiting for transfers between devices: 53.1 us -> 0.02 us  [shards(): lax.all_gather(own_rhs, 'col', axis=0, tiled=True)]
    ppermute x0 -> x15, starting transfers between devices: none -> 40.8 us  [the longest x7 38.7 us: see_limits_over_axis(): shaped = ppermute(shaped, 'col', row_list)]
    dynamic_update_slice x0 -> x16, local copies, waits for them, and re-layouts: none -> 23.6 us  [the longest x7 11.4 us: see_limits_over_axis(): lax.dynamic_update_slice_in_dim(opened, shaped, (later + num) % v_now * y...]
    another operation x15, matrix products: 38.9 us -> 23.3 us  [shards(): lax.linalg.triangular_solve(block_row[:, :block_size], block_rhs, left_si...]
    another operation x15, matrix products: 37.4 us -> 22 us  [shards(): lax.linalg.triangular_solve(block_row[:, block_size:], second_rhs, left_s...]
    dot_general x1, matrix products: 30.9 us -> 18.3 us  [shards(): jnp.dot(block_row[:, :block_size], first_block, precision=lax.Precision.H...]
  transfers between devices with their start and end apart: 8 -> 22, of which waited for: 7 -> 15; matrix products, arithmetic and copies ran while one was open for 15% -> 31% of each run, Pallas kernels for 0% -> 0%
where the time goes in v1:
time: 839 us; the launch traced here: 830 us
  waiting for transfers between devices  435 us (52%)
  other arithmetic  174 us (21%)
  matrix products  88.3 us (11%)
  local copies, waits for them, and re-layouts  77.9 us (9%)
  starting transfers between devices  41.1 us (5%)
  between operations  14 us (2%)
    reduce_scatter x4, waiting for transfers between devices, reduce_turn(): lax.psum_scatter(partial_value, 'col', scatter_dimension=0, tiled=True)  301 us
    another operation x2, other arithmetic, shards(): lax.linalg.triangular_solve(block_row[:, block_size:], second_rhs, left_s...  86.5 us
    another operation x2, other arithmetic, shards(): lax.linalg.triangular_solve(block_row[:, :block_size], block_rhs, left_si...  78.8 us
    psum x2, waiting for transfers between devices, broadcast(): return lax.psum(jnp.where(mine, x, jnp.zeros_like(x)), axis)  69 us
    ppermute x8, waiting for transfers between devices, see_limits_over_axis(): all_rows = ppermute(all_rows, 'col', rack)  54.8 us
    ppermute x7, starting transfers between devices, see_limits_over_axis(): shaped = ppermute(shaped, 'col', row_list)  38.7 us
    dot_general x4, matrix products, shards(): jnp.dot(local_factor[turn_id], my_rows, precision=lax.Precision.HIGHEST)  24.8 us
    another operation x24, local copies, waits for them, and re-layouts, shards(): lax.linalg.triangular_solve(block_row[:, block_size:], second_rhs, left_s...  24 us
  transfers between devices with their start and end apart: 22, of which 15 were waited for; matrix products, arithmetic and copies ran while one was open for 31% of the time, Pallas kernels for 0%

profile of v1, /device:TPU:0, one launch (start us, length us, event | category | flops | bytes accessed | tf_op | source)
XLA Modules:
  0.0 830.0 jit_solution(14582387666143403638)
XLA Ops:
  7.6 2.1 collective-permute-start
  11.4 4.7 collective-permute-start.1
  16.1 10.1 %collective-permute-done = f32[1024,128]{1,0:T(8,128)S(1)} collective-permute-done((f32[1024,128]{1,0:T(8,128)S(1)}, f32[1024,128]{1,0:T(8,128)S(1)}, u32[]{:S(2)}, u32[]{:S(2)}) %collective-permute-start) | collective-permute-done | bytes 524320 | tf_op jit(solution)/shard_map/ppermute | solution.py:34
  26.2 2.7 collective-permute-done.1
  28.9 5.8 collective-permute-start.3
  34.7 10.7 %collective-permute-done.2 = f32[1024,128]{1,0:T(8,128)S(1)} collective-permute-done((f32[1024,128]{1,0:T(8,128)S(1)}, f32[1024,128]{1,0:T(8,128)S(1)}, u32[]{:S(2)}, u32[]{:S(2)}) %collective-permute-start.2) | collective-permute-done | bytes 524320 | tf_op jit(solution)/shard_map/ppermute | solution.py:34
  45.7 5.8 collective-permute-start.5
  51.5 13.5 %collective-permute-done.4 = f32[1024,128]{1,0:T(8,128)S(1)} collective-permute-done((f32[1024,128]{1,0:T(8,128)S(1)}, f32[1024,128]{1,0:T(8,128)S(1)}, u32[]{:S(2)}, u32[]{:S(2)}) %collective-permute-start.4) | collective-permute-done | bytes 524320 | tf_op jit(solution)/shard_map/ppermute | solution.py:34
  65.0 7.0 collective-permute-done.5
  72.1 5.9 collective-permute-start.7
  78.0 11.5 %collective-permute-done.6 = f32[1024,128]{1,0:T(8,128)} collective-permute-done((f32[1024,128]{1,0:T(8,128)S(1)}, f32[1024,128]{1,0:T(8,128)}, u32[]{:S(2)}, u32[]{:S(2)}) %collective-permute-start.6) | collective-permute-done | bytes 524320 | tf_op jit(solution)/shard_map/ppermute | solution.py:34
  89.6 5.9 collective-permute-start.9
  95.4 4.3 broadcast_in_dim.9
  100.7 2.1 collective-permute-done.8
  105.6 2.0 constant_dynamic-update-slice_fusion.62
  107.6 5.4 collective-permute-start.11
  116.5 2.0 constant_dynamic-update-slice_fusion.59
  118.5 1.9 constant_dynamic-update-slice_fusion.58
  120.4 1.9 constant_dynamic-update-slice_fusion.57
  122.3 5.3 collective-permute-start.13
  136.0 6.0 collective-permute-done.14
  143.0 7.9 slice_select_fusion
  150.9 23.2 %while.4 = (s32[]{:T(128)}, f32[1024,1024]{1,0:T(8,128)}, s32[8,2]{0,1:T(2,128)S(1)}, f32[8,128,128]{2,1,0:T(8,128)S(1)}, s32[]{:T(128)}) while((s32[]{:T(128)}, f32[1024,1024]{1,0:T(8,128)}, s32[8,2]{0,1:T(2,128)S(1)}, f32[8,128,128]{2,1,0:T(8,128)S(1)}, s32[]{:T(128)}) %tuple.80), condition=%wide.while_cond, body=%wide.while_body.sunk | while | flops 2 | bytes 131181 | solution.py:54
  151.5 2.3 bitcast_dynamic-update-slice_fusion.4
  154.4 2.3 bitcast_dynamic-update-slice_fusion.4
  157.3 2.3 bitcast_dynamic-update-slice_fusion.4
  160.3 2.3 bitcast_dynamic-update-slice_fusion.4
  163.2 2.3 bitcast_dynamic-update-slice_fusion.4
  166.1 2.3 bitcast_dynamic-update-slice_fusion.4
  169.0 2.3 bitcast_dynamic-update-slice_fusion.4
  171.9 2.2 bitcast_dynamic-update-slice_fusion.4
  174.1 78.8 %custom-call.4 = f32[8,128,128]{1,2,0:T(8,128)S(1)} custom-call(f32[8,128,128]{2,1,0:T(8,128)S(1)} %get-tuple-element.20), custom_call_target="InvertDiagBlocksLowerTriangular" | custom-call | tf_op jit(solution)/shard_map/triangular_solve/custom-call.1 | solution.py:54
  259.7 2.0 fusion.34
  262.5 2.2 fusion.37
  265.4 2.6 convolution_subtract_fusion.2
  268.7 2.8 convolution_subtract_fusion.1
  272.2 3.5 convolution_subtract_fusion.3
  276.3 2.5 broadcast_select_fusion.1
  278.9 24.2 %while.5 = (s32[]{:T(128)}, f32[1024,1024]{1,0:T(8,128)}, s32[8,2]{0,1:T(2,128)S(1)}, f32[8,128,128]{2,1,0:T(8,128)S(1)}, s32[]{:T(128)}) while((s32[]{:T(128)}, f32[1024,1024]{1,0:T(8,128)}, s32[8,2]{0,1:T(2,128)S(1)}, f32[8,128,128]{2,1,0:T(8,128)S(1)}, s32[]{:T(128)}) %tuple.100), condition=%wide.while_cond.clone, body=%wide.while_body.clone.sunk | while | flops 2 | bytes 131181 | solution.py:61
  279.6 2.3 bitcast_dynamic-update-slice_fusion.5
  282.6 2.3 bitcast_dynamic-update-slice_fusion.5
  285.7 2.3 bitcast_dynamic-update-slice_fusion.5
  288.7 2.3 bitcast_dynamic-update-slice_fusion.5
  291.7 2.3 bitcast_dynamic-update-slice_fusion.5
  294.7 2.3 bitcast_dynamic-update-slice_fusion.5
  297.8 2.3 bitcast_dynamic-update-slice_fusion.5
  300.8 2.3 bitcast_dynamic-update-slice_fusion.5
  303.1 78.6 %custom-call.5 = f32[8,128,128]{1,2,0:T(8,128)S(1)} custom-call(f32[8,128,128]{2,1,0:T(8,128)S(1)} %get-tuple-element.21), custom_call_target="InvertDiagBlocksLowerTriangular" | custom-call | tf_op jit(solution)/shard_map/triangular_solve/custom-call.1 | solution.py:61
  381.7 18.3 %fusion.19 = f32[1024,1024]{1,0:T(8,128)S(1)} fusion(f32[1024,1024]{1,0:T(8,128)} %all-reduce.3.cloned.1.call-done, f32[1024,2048]{1,0:T(8,128)} %constant_dynamic-update-slice_fusion.50, f32[1,1,1024,1024]{3,2,1,0:T(8,128)} %all-gather.3.cloned.1.call-done), kind=kOutput, calls=%fused_computation.33 | convolution fusion | flops 12885950464 | bytes 16777216 | tf_op jit(solution)/shard_map/dot_general | solution.py:58
  405.4 2.0 fusion.28
  408.2 2.2 fusion.11
  411.1 2.6 fusion.70
  414.5 2.8 fusion.67
  418.0 3.4 fusion.64
  422.1 2.5 broadcast_select_fusion
  424.6 69.0 %all-reduce.5.cloned.1.call-done = f32[1024,1024]{1,0:T(8,128)} async-done(((f32[1024,1024]{1,0:T(8,128)}), f32[1024,1024]{1,0:T(8,128)}) %all-reduce.5.cloned.1.call-update) | async-done | bytes 4194320 | tf_op jit(solution)/shard_map/psum | solution.py:10
  493.6 6.2 convolution_bitcast_fusion.3
  499.9 6.2 convolution_bitcast_fusion.2
  506.1 6.1 convolution_bitcast_fusion.1
  512.4 6.2 convolution_bitcast_fusion
  518.6 59.2 %reduce-scatter.5.cloned.1.call-done = f32[64,1024]{1,0:T(8,128)} async-done(((f32[1024,1024]{1,0:T(8,128)}), f32[64,1024]{1,0:T(8,128)}) %reduce-scatter.5.cloned.1.call-update) | async-done | bytes 262160 | tf_op jit(solution)/shard_map/reduce_scatter | solution.py:18
  577.8 80.6 %reduce-scatter.7.cloned.1.call-done = f32[64,1024]{1,0:T(8,128)} async-done(((f32[1024,1024]{1,0:T(8,128)}), f32[64,1024]{1,0:T(8,128)}) %reduce-scatter.7.cloned.1.call-update) | async-done | bytes 262160 | tf_op jit(solution)/shard_map/reduce_scatter | solution.py:18
  658.4 80.3 %reduce-scatter.9.cloned.1.call-done = f32[64,1024]{1,0:T(8,128)} async-done(((f32[1024,1024]{1,0:T(8,128)}), f32[64,1024]{1,0:T(8,128)}) %reduce-scatter.9.cloned.1.call-update) | async-done | bytes 262160 | tf_op jit(solution)/shard_map/reduce_scatter | solution.py:18
  738.6 80.8 %reduce-scatter.11.cloned.1.call-done = f32[64,1024]{1,0:T(8,128)} async-done(((f32[1024,1024]{1,0:T(8,128)}), f32[64,1024]{1,0:T(8,128)}) %reduce-scatter.11.cloned.1.call-update) | async-done | bytes 262160 | tf_op jit(solution)/shard_map/reduce_scatter | solution.py:18
  (116 shorter events, 52.7 us)
Async XLA Ops:
  6.5 246.4 %all-gather.3.cloned.1.call-start = ((), (), s32[]{:S(2)}) async-start(), calls=%async_computation.10 | async-start | bytes 4456448 | tf_op jit(solution)/shard_map/all_gather | solution.py:51
  7.6 18.6 %collective-permute-start = (f32[1024,128]{1,0:T(8,128)S(1)}, f32[1024,128]{1,0:T(8,128)S(1)}, u32[]{:S(2)}, u32[]{:S(2)}) collective-permute-start(f32[1024,128]{1,0:T(8,128)S(1)} %slice_bitcast_fusion), channel_id=1, source_target_pairs={{0,1},{1,2},{2,3},{3,4},{4,5},{5,6},{6,7},{7,8},{8,9},{9,10},{10,1... | collective-permute-start | bytes 1572872 | tf_op jit(solution)/shard_map/ppermute | solution.py:34
  11.4 370.3 %all-reduce.3.cloned.1.call-start = ((), (), s32[]{:S(2)}) async-start(), calls=%async_computation.4 | async-start | bytes 8388608 | tf_op jit(solution)/shard_map/psum | solution.py:10
  11.4 17.4 %collective-permute-start.1 = (f32[1024,128]{1,0:T(8,128)S(1)}, f32[1024,128]{1,0:T(8,128)S(1)}, u32[]{:S(2)}, u32[]{:S(2)}) collective-permute-start(f32[1024,128]{1,0:T(8,128)S(1)} %slice_bitcast_fusion), channel_id=1, source_target_pairs={{0,15},{1,0},{2,1},{3,2},{4,3},{5,4},{6,5},{7,6},{8,7},{9,8},{10,9... | collective-permute-start | bytes 1572872 | tf_op jit(solution)/shard_map/ppermute | solution.py:39
  26.2 19.2 %collective-permute-start.2 = (f32[1024,128]{1,0:T(8,128)S(1)}, f32[1024,128]{1,0:T(8,128)S(1)}, u32[]{:S(2)}, u32[]{:S(2)}) collective-permute-start(f32[1024,128]{1,0:T(8,128)S(1)} %collective-permute-done), channel_id=1, source_target_pairs={{0,1},{1,2},{2,3},{3,4},{4,5},{5,6},{6,7},{7,8},{8,9},{9,10},{10,1... | collective-permute-start | bytes 1572872 | tf_op jit(solution)/shard_map/ppermute | solution.py:34
  28.9 60.6 %copy-start.3 = (f32[1024,128]{1,0:T(8,128)}, f32[1024,128]{1,0:T(8,128)S(1)}, u32[]{:S(2)}) copy-start(f32[1024,128]{1,0:T(8,128)S(1)} %collective-permute-done.1) | copy-start | bytes 1572868
  28.9 16.8 %collective-permute-start.3 = (f32[1024,128]{1,0:T(8,128)S(1)}, f32[1024,128]{1,0:T(8,128)S(1)}, u32[]{:S(2)}, u32[]{:S(2)}) collective-permute-start(f32[1024,128]{1,0:T(8,128)S(1)} %collective-permute-done.1), channel_id=1, source_target_pairs={{0,15},{1,0},{2,1},{3,2},{4,3},{5,4},{6,5},{7,6},{8,7},{9,8},{10,9... | collective-permute-start | bytes 1572872 | tf_op jit(solution)/shard_map/ppermute | solution.py:39
  45.4 44.1 %copy-start.5 = (f32[1024,128]{1,0:T(8,128)}, f32[1024,128]{1,0:T(8,128)S(1)}, u32[]{:S(2)}) copy-start(f32[1024,128]{1,0:T(8,128)S(1)} %collective-permute-done.2) | copy-start | bytes 1572868
  45.4 19.6 %collective-permute-start.4 = (f32[1024,128]{1,0:T(8,128)S(1)}, f32[1024,128]{1,0:T(8,128)S(1)}, u32[]{:S(2)}, u32[]{:S(2)}) collective-permute-start(f32[1024,128]{1,0:T(8,128)S(1)} %collective-permute-done.2), channel_id=1, source_target_pairs={{0,1},{1,2},{2,3},{3,4},{4,5},{5,6},{6,7},{7,8},{8,9},{9,10},{10,1... | collective-permute-start | bytes 1572872 | tf_op jit(solution)/shard_map/ppermute | solution.py:34
  45.7 43.8 %copy-start.4 = (f32[1024,128]{1,0:T(8,128)}, f32[1024,128]{1,0:T(8,128)S(1)}, u32[]{:S(2)}) copy-start(f32[1024,128]{1,0:T(8,128)S(1)} %collective-permute-done.3) | copy-start | bytes 1572868
  45.7 26.4 %collective-permute-start.5 = (f32[1024,128]{1,0:T(8,128)S(1)}, f32[1024,128]{1,0:T(8,128)}, u32[]{:S(2)}, u32[]{:S(2)}) collective-permute-start(f32[1024,128]{1,0:T(8,128)S(1)} %collective-permute-done.3), channel_id=1, source_target_pairs={{0,15},{1,0},{2,1},{3,2},{4,3},{5,4},{6,5},{7,6},{8,7},{9,8},{10,9... | collective-permute-start | bytes 1572872 | tf_op jit(solution)/shard_map/ppermute | solution.py:39
  65.0 24.5 %collective-permute-start.6 = (f32[1024,128]{1,0:T(8,128)S(1)}, f32[1024,128]{1,0:T(8,128)}, u32[]{:S(2)}, u32[]{:S(2)}) collective-permute-start(f32[1024,128]{1,0:T(8,128)S(1)} %collective-permute-done.4), channel_id=1, source_target_pairs={{0,1},{1,2},{2,3},{3,4},{4,5},{5,6},{6,7},{7,8},{8,9},{9,10},{10,1... | collective-permute-start | bytes 1572872 | tf_op jit(solution)/shard_map/ppermute | solution.py:34
  72.1 17.5 %collective-permute-start.7 = (f32[1024,128]{1,0:T(8,128)}, f32[1024,128]{1,0:T(8,128)}, u32[]{:S(2)}, u32[]{:S(2)}) collective-permute-start(f32[1024,128]{1,0:T(8,128)} %collective-permute-done.5), channel_id=1, source_target_pairs={{0,15},{1,0},{2,1},{3,2},{4,3},{5,4},{6,5},{7,6},{8,7},{9,8},{10,9... | collective-permute-start | bytes 1572872 | tf_op jit(solution)/shard_map/ppermute | solution.py:39
  89.5 13.3 %collective-permute-start.8 = (f32[1024,128]{1,0:T(8,128)}, f32[1024,128]{1,0:T(8,128)}, u32[]{:S(2)}, u32[]{:S(2)}) collective-permute-start(f32[1024,128]{1,0:T(8,128)} %collective-permute-done.6), channel_id=1, source_target_pairs={{0,1},{1,2},{2,3},{3,4},{4,5},{5,6},{6,7},{7,8},{8,9},{9,10},{10,1... | collective-permute-start | bytes 1572872 | tf_op jit(solution)/shard_map/ppermute | solution.py:34
  89.5 10.3 %copy-start.1 = (f32[4,1,1024,128]{3,2,1,0:T(8,128)S(1)}, f32[4,1,1024,128]{3,2,1,0:T(8,128)}, u32[]{:S(2)}) copy-start(f32[4,1,1024,128]{3,2,1,0:T(8,128)} %param.4) | copy-start | bytes 6291460
  89.6 18.0 %collective-permute-start.9 = (f32[1024,128]{1,0:T(8,128)}, f32[1024,128]{1,0:T(8,128)}, u32[]{:S(2)}, u32[]{:S(2)}) collective-permute-start(f32[1024,128]{1,0:T(8,128)} %collective-permute-done.7), channel_id=1, source_target_pairs={{0,15},{1,0},{2,1},{3,2},{4,3},{5,4},{6,5},{7,6},{8,7},{9,8},{10,9... | collective-permute-start | bytes 1572872 | tf_op jit(solution)/shard_map/ppermute | solution.py:39
  102.8 12.8 %collective-permute-start.10 = (f32[1024,128]{1,0:T(8,128)}, f32[1024,128]{1,0:T(8,128)}, u32[]{:S(2)}, u32[]{:S(2)}) collective-permute-start(f32[1024,128]{1,0:T(8,128)} %collective-permute-done.8), channel_id=1, source_target_pairs={{0,1},{1,2},{2,3},{3,4},{4,5},{5,6},{6,7},{7,8},{8,9},{9,10},{10,1... | collective-permute-start | bytes 1572872 | tf_op jit(solution)/shard_map/ppermute | solution.py:34
  107.6 14.7 %collective-permute-start.11 = (f32[1024,128]{1,0:T(8,128)}, f32[1024,128]{1,0:T(8,128)S(1)}, u32[]{:S(2)}, u32[]{:S(2)}) collective-permute-start(f32[1024,128]{1,0:T(8,128)} %collective-permute-done.9), channel_id=1, source_target_pairs={{0,15},{1,0},{2,1},{3,2},{4,3},{5,4},{6,5},{7,6},{8,7},{9,8},{10,9... | collective-permute-start | bytes 1572872 | tf_op jit(solution)/shard_map/ppermute | solution.py:39
  115.6 13.9 %collective-permute-start.12 = (f32[1024,128]{1,0:T(8,128)}, f32[1024,128]{1,0:T(8,128)S(1)}, u32[]{:S(2)}, u32[]{:S(2)}) collective-permute-start(f32[1024,128]{1,0:T(8,128)} %collective-permute-done.10), channel_id=1, source_target_pairs={{0,1},{1,2},{2,3},{3,4},{4,5},{5,6},{6,7},{7,8},{8,9},{9,10},{10,1... | collective-permute-start | bytes 1572872 | tf_op jit(solution)/shard_map/ppermute | solution.py:34
  122.3 12.8 %collective-permute-start.13 = (f32[1024,128]{1,0:T(8,128)S(1)}, f32[1024,128]{1,0:T(8,128)S(1)}, u32[]{:S(2)}, u32[]{:S(2)}) collective-permute-start(f32[1024,128]{1,0:T(8,128)S(1)} %collective-permute-done.11), channel_id=1, source_target_pairs={{0,15},{1,0},{2,1},{3,2},{4,3},{5,4},{6,5},{7,6},{8,7},{9,8},{10,9... | collective-permute-start | bytes 1572872 | tf_op jit(solution)/shard_map/ppermute | solution.py:39
  129.5 12.5 %collective-permute-start.14 = (f32[1024,128]{1,0:T(8,128)S(1)}, f32[1024,128]{1,0:T(8,128)S(1)}, u32[]{:S(2)}, u32[]{:S(2)}) collective-permute-start(f32[1024,128]{1,0:T(8,128)S(1)} %collective-permute-done.12), channel_id=1, source_target_pairs={{0,1},{1,2},{2,3},{3,4},{4,5},{5,6},{6,7},{7,8},{8,9},{9,10},{10,1... | collective-permute-start | bytes 1572872 | tf_op jit(solution)/shard_map/ppermute | solution.py:34
  252.9 4.3 copy-start
  278.8 214.8 %all-reduce.5.cloned.1.call-start = ((), (), s32[]{:S(2)}) async-start(), calls=%async_computation.5 | async-start | bytes 8388608 | tf_op jit(solution)/shard_map/psum | solution.py:10
  424.6 153.2 %reduce-scatter.5.cloned.1.call-start = ((), (), s32[]{:S(2)}) async-start(), calls=%async_computation.6 | async-start | bytes 4456448 | tf_op jit(solution)/shard_map/reduce_scatter | solution.py:18
  499.8 158.5 %reduce-scatter.7.cloned.1.call-start = ((), (), s32[]{:S(2)}) async-start(), calls=%async_computation.7 | async-start | bytes 4456448 | tf_op jit(solution)/shard_map/reduce_scatter | solution.py:18
  506.1 232.5 %reduce-scatter.9.cloned.1.call-start = ((), (), s32[]{:S(2)}) async-start(), calls=%async_computation.8 | async-start | bytes 4456448 | tf_op jit(solution)/shard_map/reduce_scatter | solution.py:18
  512.3 307.1 %reduce-scatter.11.cloned.1.call-start = ((), (), s32[]{:S(2)}) async-start(), calls=%async_computation.9 | async-start | bytes 4456448 | tf_op jit(solution)/shard_map/reduce_scatter | solution.py:18
  518.6 300.8 %copy-start.2 = (f32[4,1,64,1024]{3,2,1,0:T(8,128)S(1)}, f32[4,1,64,1024]{3,2,1,0:T(8,128)}, u32[]{:S(2)}) copy-start(f32[4,1,64,1024]{3,2,1,0:T(8,128)} %param.5) | copy-start | bytes 3145732
Sparse Core Ops, SparseCore 0:
  11.5 77.0 all-gather.2
  279.0 69.2 all-reduce.2
  424.7 68.8 all-reduce.4
  499.9 77.8 reduce-scatter.4
  581.3 76.9 reduce-scatter.6
  661.6 77.0 reduce-scatter.8
  742.3 77.0 reduce-scatter.10
